TPU v7x, 512 devices: a whole 4x4x16 slice. The times are simulated.
512 devices in a mesh: section: 16 (over z), expert: 8 (over y, core), dp: 4 (over x).
Axes of the slice: x: 4, y: 4, z: 16, core: 2. Of those that a mesh axis runs over, the one named last changes fastest.
Arguments:
- tokens: bfloat16 [1024, 3072], P('expert', 'dp'), may hold values from -6 to 6
- expert_ids: int32 [1024, 2], P('expert'), may hold values from 0 to 7, all different within a row; in each aligned block of 128 rows (0 to 127, 128 to 255, ...) at most 64 rows name the same one
- w_gate: bfloat16 [8, 3072, 8192], P('expert', 'dp', 'section'), may hold values from -0.109375 to 0.109375
- w_up: bfloat16 [8, 3072, 8192], P('expert', 'dp', 'section'), may hold values from -0.109375 to 0.109375
- cotangent: bfloat16 [8, 512, 8192], P('expert', None, 'section'), may hold values from -6 to 6
Outputs:
- acted: bfloat16 [8, 512, 8192], P('expert', None, 'section')
- input_grad: bfloat16 [1024, 3072], P('expert', 'dp')
- gate_grad: bfloat16 [8, 3072, 8192], P('expert', 'dp', 'section')
- up_grad: bfloat16 [8, 3072, 8192], P('expert', 'dp', 'section')
Inputs may be any that keep to these rules, and one draw needn't show every extreme that they name: `expert_ids`: each token names two different experts. Among the 128 tokens of one index of the expert axis no expert is named more than 64 times, a bound that some block reaches.
All inputs are finite; a program needn't handle non-finite values.
Results may differ from a plain program's by a relative error of at most 0.0049.
Values may be sent and summed in bfloat16 or wider, within the bound.
A program may use at most 64 MiB of HBM per device.

v0:
```python
import jax
import jax.numpy as jnp
from jax import lax
from jax.sharding import PartitionSpec as P


def local(tokens, expert_ids, w_gate, w_up, cotangent):
    rows, width = tokens.shape
    experts = lax.axis_size("expert")
    capacity = min(rows, 4 * rows // experts)
    wg = w_gate[0]
    wu = w_up[0]
    flat_ids = expert_ids.reshape(-1)
    member = (flat_ids[:, None] == jnp.arange(experts, dtype=jnp.int32)[None, :]).astype(jnp.int32)
    rank = jnp.sum((jnp.cumsum(member, axis=0) - member) * member, axis=1)
    slot = flat_ids * capacity + rank
    token_of = jnp.arange(2 * rows, dtype=jnp.int32) // 2
    source = jnp.full((experts * capacity,), rows, jnp.int32).at[slot].set(token_of)
    occupied = jnp.zeros((experts * capacity,), jnp.bfloat16).at[slot].set(1.0)
    x_pad = jnp.concatenate([tokens, jnp.zeros((1, width), jnp.bfloat16)], axis=0)
    send_x = jnp.take(x_pad, source, axis=0).reshape(experts, capacity, width)
    recv_x, recv_live = (
        lax.all_to_all(send_x, "expert", split_axis=0, concat_axis=0, tiled=True),
        lax.all_to_all(
            occupied.reshape(experts, capacity), "expert", split_axis=0, concat_axis=0, tiled=True
        ),
    )
    x_rows = recv_x.reshape(-1, width)
    parts = (x_rows,)
    part_gate = jnp.dot(parts[0], wg, preferred_element_type=jnp.float32)
    part_up = jnp.dot(parts[0], wu, preferred_element_type=jnp.float32)
    pre_gate, pre_up = lax.psum((part_gate, part_up), "dp")
    sig = jax.nn.sigmoid(pre_gate)
    silu_v = pre_gate * sig
    acted = (silu_v * pre_up).astype(jnp.bfloat16)
    cf = cotangent[0].astype(jnp.float32)
    gate_part = (cf * pre_up * sig * (1.0 + pre_gate * (1.0 - sig))).astype(jnp.bfloat16)
    up_part = (cf * silu_v).astype(jnp.bfloat16)
    contract = (((0,), (0,)), ((), ()))
    gate_grad = lax.dot_general(x_rows, gate_part, contract, preferred_element_type=jnp.float32)
    up_grad = lax.dot_general(x_rows, up_part, contract, preferred_element_type=jnp.float32)
    parts = (gate_part, up_part)
    back = lax.dot_general(
        parts[0], wg, (((1,), (1,)), ((), ())), preferred_element_type=jnp.float32
    ) + lax.dot_general(parts[1], wu, (((1,), (1,)), ((), ())), preferred_element_type=jnp.float32)
    back = (back,)[0]
    whole = lax.psum(back, "section")
    home = lax.all_to_all(
        whole.reshape(experts, capacity, width), "expert", split_axis=0, concat_axis=0, tiled=True
    )
    token_grad = jnp.sum(
        jnp.take(home.reshape(-1, width), slot, axis=0).reshape(rows, 2, width), axis=1
    )
    return (
        acted[None],
        token_grad.astype(jnp.bfloat16),
        gate_grad.astype(jnp.bfloat16)[None],
        up_grad.astype(jnp.bfloat16)[None],
    )


def solution(mesh):
    placed = (
        P("expert", "dp"),
        P("expert", None),
        P("expert", "dp", "section"),
        P("expert", "dp", "section"),
        P("expert", None, "section"),
    )
    return jax.shard_map(
        local,
        mesh=mesh,
        in_specs=placed,
        out_specs=(
            P("expert", None, "section"),
            P("expert", "dp"),
            P("expert", "dp", "section"),
            P("expert", "dp", "section"),
        ),
        check_vma=False,
    )
```

profile of v0, /device:TPU:1, one launch (start us, length us, event | category | flops | bytes accessed | tf_op | source)
XLA Modules:
  0.0 297.3 jit_solution(851770255115678732)
XLA Ops:
  7.2 0.0 copy-start
  7.2 0.0 all-reduce.7.cloned.1.call-start
  7.2 0.7 broadcast_multiply_fusion
  8.0 0.8 copy.14
  8.8 0.1 eq.29
  8.9 0.1 eq.25
  9.0 0.1 copy.13
  9.2 0.1 mul.45
  9.3 0.6 reduce-window.6
  9.9 0.2 slice_reduce_fusion
  10.2 0.1 fusion.16
  10.3 1.4 scatter_custom_fusion
  11.7 0.1 broadcast_in_dim.40
  11.8 0.9 concatenate.3
  12.7 2.0 gather_fusion
  14.8 0.0 copy-start.4
  14.8 0.1 broadcast_select_fusion
  14.9 21.5 %all_to_all.10 = bf16[8,64,768]{2,1,0:T(8,128)(2,1)S(1)} all-to-all(bf16[8,64,768]{2,1,0:T(8,128)(2,1)S(1)} %broadcast_select_fusion), channel_id=1, replica_groups=mesh['section'=16,'expert'=8,'dp'=4] {'expert'}, dimensions={0} | all-to-all | bytes 1572864 | tf_op jit(solution)/shard_map/all_to_all | solution.py:23
  36.4 0.0 copy-done.4
  36.4 1.6 fusion.8
  38.1 0.0 copy-done
  38.1 1.6 fusion.12
  39.6 0.0 copy-start.6
  39.6 0.0 all-reduce.7.cloned.1.call-update
  39.6 0.0 all-reduce.5.cloned.1.call-start
  39.7 73.3 %all-reduce.7.cloned.1.call-done = (f32[512,512]{1,0:T(8,128)}, f32[512,512]{1,0:T(8,128)}) async-done(((f32[512,512]{1,0:T(8,128)}, f32[512,512]{1,0:T(8,128)}), (f32[512,512]{1,0:T(8,128)}, f32[512,512]{1,0:T(8,128)})) %all-reduce.7.cloned.1.call-update) | async-done | bytes 2097168 | tf_op jit(solution)/shard_map/psum | solution.py:32
  113.0 0.0 copy-done.6
  113.0 2.9 fusion.4
  115.9 0.0 copy-start.1
  115.9 0.0 copy-start.2
  115.9 0.0 copy-start.5
  115.9 0.0 copy-start.7
  115.9 0.6 fusion.10
  116.5 0.8 copy-done.2
  117.3 0.2 copy-done.5
  117.5 0.1 copy-done.7
  117.7 1.9 convolution_add_fusion
  119.6 0.0 copy-done.1
  119.6 0.0 all-reduce.5.cloned.1.call-update
  119.6 0.0 copy-start.9
  119.7 132.2 %all-reduce.5.cloned.1.call-done = f32[8,64,768]{2,1,0:T(8,128)} async-done(((f32[8,64,768]{2,1,0:T(8,128)}), f32[8,64,768]{2,1,0:T(8,128)}) %all-reduce.5.cloned.1.call-update) | async-done | bytes 1572880 | tf_op jit(solution)/shard_map/psum | solution.py:47
  251.8 14.7 %all-to-all-start.1 = ((f32[8,64,768]{2,1,0:T(8,128)}), f32[8,64,768]{2,1,0:T(8,128)S(1)}, u32[]{:S(2)}, u32[]{:S(2)}) async-start(f32[8,64,768]{2,1,0:T(8,128)} %all-reduce.5.cloned.1.call-done), calls=%async_computation.1 | async-start | bytes 3145728 | tf_op jit(solution)/shard_map/all_to_all | solution.py:48
  266.5 0.1 reduce_sum.24
  266.7 0.1 copy.16
  266.7 0.0 copy-done.9
  266.7 0.1 copy.17
  266.9 0.0 copy-start.3
  266.9 0.0 copy-start.8
  266.9 2.6 fusion
  269.6 0.0 copy-done.3
  269.6 0.0 copy-done.8
  269.6 1.6 fusion.1
  271.2 15.9 %all-to-all-done.1 = f32[8,64,768]{2,1,0:T(8,128)S(1)} async-done(((f32[8,64,768]{2,1,0:T(8,128)}), f32[8,64,768]{2,1,0:T(8,128)S(1)}, u32[]{:S(2)}, u32[]{:S(2)}) %all-to-all-start.1) | async-done | bytes 1572896 | tf_op jit(solution)/shard_map/all_to_all | solution.py:48
  287.1 1.1 gather_fusion.1
  288.2 0.5 gather.15
  288.7 1.8 select_reduce_fusion
  (10 shorter events, 0.1 us)
Async XLA Ops:
  7.2 30.9 %copy-start = (bf16[1,768,512]{2,1,0:T(8,128)(2,1)S(1)}, bf16[1,768,512]{2,1,0:T(8,128)(2,1)}, u32[]{:S(2)}) copy-start(bf16[1,768,512]{2,1,0:T(8,128)(2,1)} %param.7) | copy-start | bytes 2359300
  7.2 105.8 %all-reduce.7.cloned.1.call-start = ((), (), s32[]{:S(2)}) async-start(), calls=%async_computation.3 | async-start | bytes 4194304 | tf_op jit(solution)/shard_map/psum | solution.py:32
  14.8 21.7 %copy-start.4 = (bf16[1,768,512]{2,1,0:T(8,128)(2,1)S(1)}, bf16[1,768,512]{2,1,0:T(8,128)(2,1)}, u32[]{:S(2)}) copy-start(bf16[1,768,512]{2,1,0:T(8,128)(2,1)} %param.8) | copy-start | bytes 2359300
  39.6 73.4 %copy-start.6 = (bf16[1,512,512]{2,1,0:T(8,128)(2,1)S(1)}, bf16[1,512,512]{2,1,0:T(8,128)(2,1)}, u32[]{:S(2)}) copy-start(bf16[1,512,512]{2,1,0:T(8,128)(2,1)} %param.9) | copy-start | bytes 1572868
  39.6 212.2 %all-reduce.5.cloned.1.call-start = ((), (), s32[]{:S(2)}) async-start(), calls=%async_computation.2 | async-start | bytes 3145728 | tf_op jit(solution)/shard_map/psum | solution.py:47
  115.9 3.7 %copy-start.1 = (bf16[512,512]{1,0:T(8,128)(2,1)}, bf16[512,512]{1,0:T(8,128)(2,1)S(1)}, u32[]{:S(2)}) copy-start(bf16[512,512]{1,0:T(8,128)(2,1)S(1)} %get-tuple-element.6) | copy-start | bytes 1572868
  115.9 1.4 copy-start.2
  115.9 1.6 copy-start.5
  115.9 1.8 copy-start.7
  119.6 147.1 %copy-start.9 = (s32[128,2]{0,1:T(2,128)S(1)}, s32[128,2]{0,1:T(2,128)}, u32[]{:S(2)}) copy-start(s32[128,2]{0,1:T(2,128)} %param.6) | copy-start | bytes 3076
  251.8 35.3 %all-to-all-start.1 = ((f32[8,64,768]{2,1,0:T(8,128)}), f32[8,64,768]{2,1,0:T(8,128)S(1)}, u32[]{:S(2)}, u32[]{:S(2)}) async-start(f32[8,64,768]{2,1,0:T(8,128)} %all-reduce.5.cloned.1.call-done), calls=%async_computation.1 | async-start | bytes 3145728 | tf_op jit(solution)/shard_map/all_to_all | solution.py:48
  266.9 2.7 copy-start.3
  266.9 2.7 copy-start.8
Sparse Core Ops, SparseCore 0:
  39.8 73.2 all-reduce.6
  119.8 132.0 all-reduce.4
where the time goes:
time: 298 us; the launch traced here: 297 us
  waiting for transfers between devices  221 us (74%)
  blocking collectives  21.5 us (7%)
  starting transfers between devices  14.8 us (5%)
  between operations  14.2 us (5%)
  matrix products  9.94 us (3%)
  local copies, waits for them, and re-layouts  9.07 us (3%)
  other arithmetic  6.29 us (2%)
    psum x1, waiting for transfers between devices, local(): whole = lax.psum(back, 'section')  132 us
    psum x1, waiting for transfers between devices, local(): pre_gate, pre_up = lax.psum((part_gate, part_up), 'dp')  73.3 us
    all_to_all x1, blocking collectives, local(): lax.all_to_all(send_x, 'expert', split_axis=0, concat_axis=0, tiled=True)  21.5 us
    all_to_all x1, waiting for transfers between devices, local(): lax.all_to_all(whole.reshape(experts, capacity, width), 'expert', split_a...  15.9 us
    all_to_all x1, starting transfers between devices, local(): lax.all_to_all(whole.reshape(experts, capacity, width), 'expert', split_a...  14.7 us
  transfers between devices with their start and end apart: 3, of which 3 were waited for; matrix products, arithmetic and copies ran while one was open for 2% of the time, Pallas kernels for 0%

commit v1 on v0

--- a/solution.py
+++ b/solution.py
@@ -44,7 +44,10 @@
         parts[0], wg, (((1,), (1,)), ((), ())), preferred_element_type=jnp.float32
     ) + lax.dot_general(parts[1], wu, (((1,), (1,)), ((), ())), preferred_element_type=jnp.float32)
     back = (back,)[0]
-    whole = lax.psum(back, "section")
+    chips = lax.psum(1, "section")
+    whole = back
+    for it in [[(b, b ^ h) for b in range(chips)] for h in (1, 2, 4, 8, 16) if h < chips]:
+        whole = whole + lax.ppermute(whole, perm=it, axis_name="section")
     home = lax.all_to_all(
         whole.reshape(experts, capacity, width), "expert", split_axis=0, concat_axis=0, tiled=True
     )

time: 298 us -> 549 us (1.84)
  the two profiles are of different devices: /device:TPU:1 before, /device:TPU:128 now
where the time goes in v1:
time: 549 us
  waiting for transfers between devices  463 us (84%)
  starting transfers between devices  25.9 us (5%)
  blocking collectives  17.6 us (3%)
  between operations  14.2 us (3%)
  local copies, waits for them, and re-layouts  10.7 us (2%)
  matrix products  8.76 us (2%)
  other arithmetic  8.24 us (2%)
    ppermute x4, waiting for transfers between devices, local(): whole = whole + lax.ppermute(whole, perm=it, axis_name='section')  371 us
    psum x1, waiting for transfers between devices, local(): pre_gate, pre_up = lax.psum((part_gate, part_up), 'dp')  75.2 us
    ppermute x4, starting transfers between devices, local(): whole = whole + lax.ppermute(whole, perm=it, axis_name='section')  21.5 us
    all_to_all x1, blocking collectives, local(): lax.all_to_all(send_x, 'expert', split_axis=0, concat_axis=0, tiled=True)  17.6 us
    all_to_all x1, waiting for transfers between devices, local(): lax.all_to_all(whole.reshape(experts, capacity, width), 'expert', split_a...  16.9 us
  transfers between devices with their start and end apart: 6, of which 6 were waited for; matrix products, arithmetic and copies ran while one was open for 1% of the time, Pallas kernels for 0%

profile of v1, /device:TPU:128, one launch (start us, length us, event | category | flops | bytes accessed | tf_op | source)
XLA Modules:
  0.0 548.7 jit_solution(16780759255961008246)
XLA Ops:
  7.2 0.0 copy-start
  7.2 0.0 all-reduce.4.cloned.1.call-start
  7.2 0.7 broadcast_multiply_fusion
  8.0 0.8 copy.14
  8.8 0.1 eq.29
  8.9 0.1 eq.25
  9.0 0.1 copy.13
  9.2 0.1 mul.45
  9.3 0.6 reduce-window.6
  9.9 0.2 slice_reduce_fusion
  10.2 0.1 fusion.16
  10.3 1.4 scatter_custom_fusion
  11.7 0.1 broadcast_in_dim.40
  11.8 0.9 concatenate.3
  12.7 2.0 gather_fusion
  14.8 0.0 copy-start.4
  14.8 0.1 broadcast_select_fusion
  14.9 17.6 %all_to_all.10 = bf16[8,64,768]{2,1,0:T(8,128)(2,1)S(1)} all-to-all(bf16[8,64,768]{2,1,0:T(8,128)(2,1)S(1)} %broadcast_select_fusion), channel_id=1, replica_groups=mesh['section'=16,'expert'=8,'dp'=4] {'expert'}, dimensions={0} | all-to-all | bytes 1572864 | tf_op jit(solution)/shard_map/all_to_all | solution.py:23
  32.5 0.0 copy-done.4
  32.5 1.6 fusion.8
  34.1 0.0 copy-done
  34.1 1.6 fusion.12
  35.6 0.0 copy-start.5
  35.6 0.0 all-reduce.4.cloned.1.call-update
  35.7 75.2 %all-reduce.4.cloned.1.call-done = (f32[512,512]{1,0:T(8,128)}, f32[512,512]{1,0:T(8,128)}) async-done(((f32[512,512]{1,0:T(8,128)}, f32[512,512]{1,0:T(8,128)}), (f32[512,512]{1,0:T(8,128)}, f32[512,512]{1,0:T(8,128)})) %all-reduce.4.cloned.1.call-update) | async-done | bytes 2097168 | tf_op jit(solution)/shard_map/psum | solution.py:32
  110.9 0.0 copy-done.5
  110.9 2.9 fusion.4
  113.7 0.0 copy-start.1
  113.8 0.0 copy-start.2
  113.8 0.6 fusion.10
  114.4 0.8 copy-done.2
  115.2 0.8 convolution_add_fusion
  116.0 0.0 copy-done.1
  116.0 3.5 collective-permute-start
  119.5 34.4 %collective-permute-done = f32[512,768]{1,0:T(8,128)S(1)} collective-permute-done((f32[512,768]{1,0:T(8,128)S(1)}, f32[512,768]{1,0:T(8,128)S(1)}, u32[]{:S(2)}, u32[]{:S(2)}) %collective-permute-start) | collective-permute-done | bytes 1572896 | tf_op jit(solution)/shard_map/ppermute | solution.py:50
  153.8 0.2 add.86
  154.0 4.5 collective-permute-start.1
  158.5 67.1 %collective-permute-done.1 = f32[512,768]{1,0:T(8,128)S(1)} collective-permute-done((f32[512,768]{1,0:T(8,128)S(1)}, f32[512,768]{1,0:T(8,128)S(1)}, u32[]{:S(2)}, u32[]{:S(2)}) %collective-permute-start.1) | collective-permute-done | bytes 1572896 | tf_op jit(solution)/shard_map/ppermute | solution.py:50
  225.6 0.2 add.87
  225.8 2.1 collective-permute-start.2
  227.9 167.3 %collective-permute-done.2 = f32[512,768]{1,0:T(8,128)S(1)} collective-permute-done((f32[512,768]{1,0:T(8,128)S(1)}, f32[512,768]{1,0:T(8,128)S(1)}, u32[]{:S(2)}, u32[]{:S(2)}) %collective-permute-start.2) | collective-permute-done | bytes 1572896 | tf_op jit(solution)/shard_map/ppermute | solution.py:50
  395.2 0.2 add.88
  395.4 11.4 %collective-permute-start.3 = (f32[512,768]{1,0:T(8,128)S(1)}, f32[512,768]{1,0:T(8,128)S(1)}, u32[]{:S(2)}, u32[]{:S(2)}) collective-permute-start(f32[512,768]{1,0:T(8,128)S(1)} %add.88), channel_id=1, source_target_pairs={{0,256},{32,288},{64,320},{96,352},{128,384},{160,416},{192,448},{... | collective-permute-start | bytes 4718600 | tf_op jit(solution)/shard_map/ppermute | solution.py:50
  406.8 102.3 %collective-permute-done.3 = f32[512,768]{1,0:T(8,128)S(1)} collective-permute-done((f32[512,768]{1,0:T(8,128)S(1)}, f32[512,768]{1,0:T(8,128)S(1)}, u32[]{:S(2)}, u32[]{:S(2)}) %collective-permute-start.3) | collective-permute-done | bytes 1572896 | tf_op jit(solution)/shard_map/ppermute | solution.py:50
  509.1 1.4 add.89
  510.5 0.0 copy-start.7
  510.5 4.4 all-to-all-start.1
  515.0 0.1 reduce_sum.24
  515.1 0.1 copy.16
  515.2 0.0 copy-done.7
  515.2 0.1 copy.17
  515.3 0.0 copy-start.3
  515.3 0.0 copy-start.6
  515.4 2.6 fusion
  518.0 0.0 copy-done.3
  518.0 0.0 copy-done.6
  518.0 1.6 fusion.1
  519.6 16.9 %all-to-all-done.1 = f32[8,64,768]{2,1,0:T(8,128)S(1)} async-done(((f32[8,64,768]{2,1,0:T(8,128)}), f32[8,64,768]{2,1,0:T(8,128)S(1)}, u32[]{:S(2)}, u32[]{:S(2)}) %all-to-all-start.1) | async-done | bytes 1572896 | tf_op jit(solution)/shard_map/all_to_all | solution.py:51
  536.5 2.0 gather_fusion.1
  538.5 1.6 gather.15
  540.1 1.8 select_reduce_fusion
  (10 shorter events, 0.1 us)
Async XLA Ops:
  7.2 26.9 %copy-start = (bf16[1,768,512]{2,1,0:T(8,128)(2,1)S(1)}, bf16[1,768,512]{2,1,0:T(8,128)(2,1)}, u32[]{:S(2)}) copy-start(bf16[1,768,512]{2,1,0:T(8,128)(2,1)} %param.7) | copy-start | bytes 2359300
  7.2 103.7 %all-reduce.4.cloned.1.call-start = ((), (), s32[]{:S(2)}) async-start(), calls=%async_computation.2 | async-start | bytes 4194304 | tf_op jit(solution)/shard_map/psum | solution.py:32
  14.8 17.7 %copy-start.4 = (bf16[1,768,512]{2,1,0:T(8,128)(2,1)S(1)}, bf16[1,768,512]{2,1,0:T(8,128)(2,1)}, u32[]{:S(2)}) copy-start(bf16[1,768,512]{2,1,0:T(8,128)(2,1)} %param.8) | copy-start | bytes 2359300
  35.6 75.2 %copy-start.5 = (bf16[1,512,512]{2,1,0:T(8,128)(2,1)S(1)}, bf16[1,512,512]{2,1,0:T(8,128)(2,1)}, u32[]{:S(2)}) copy-start(bf16[1,512,512]{2,1,0:T(8,128)(2,1)} %param.9) | copy-start | bytes 1572868
  113.7 2.2 copy-start.1
  113.8 1.4 copy-start.2
  116.0 37.9 %collective-permute-start = (f32[512,768]{1,0:T(8,128)S(1)}, f32[512,768]{1,0:T(8,128)S(1)}, u32[]{:S(2)}, u32[]{:S(2)}) collective-permute-start(f32[512,768]{1,0:T(8,128)S(1)} %convolution_add_fusion), channel_id=1, source_target_pairs={{0,32},{32,0},{64,96},{96,64},{128,160},{160,128},{192,224},{224,1... | collective-permute-start | bytes 4718600 | tf_op jit(solution)/shard_map/ppermute | solution.py:50
  154.0 71.6 %collective-permute-start.1 = (f32[512,768]{1,0:T(8,128)S(1)}, f32[512,768]{1,0:T(8,128)S(1)}, u32[]{:S(2)}, u32[]{:S(2)}) collective-permute-start(f32[512,768]{1,0:T(8,128)S(1)} %add.86), channel_id=1, source_target_pairs={{0,64},{32,96},{64,0},{96,32},{128,192},{160,224},{192,128},{224,1... | collective-permute-start | bytes 4718600 | tf_op jit(solution)/shard_map/ppermute | solution.py:50
  225.8 169.4 %collective-permute-start.2 = (f32[512,768]{1,0:T(8,128)S(1)}, f32[512,768]{1,0:T(8,128)S(1)}, u32[]{:S(2)}, u32[]{:S(2)}) collective-permute-start(f32[512,768]{1,0:T(8,128)S(1)} %add.87), channel_id=1, source_target_pairs={{0,128},{32,160},{64,192},{96,224},{128,0},{160,32},{192,64},{224,... | collective-permute-start | bytes 4718600 | tf_op jit(solution)/shard_map/ppermute | solution.py:50
  395.4 113.8 %collective-permute-start.3 = (f32[512,768]{1,0:T(8,128)S(1)}, f32[512,768]{1,0:T(8,128)S(1)}, u32[]{:S(2)}, u32[]{:S(2)}) collective-permute-start(f32[512,768]{1,0:T(8,128)S(1)} %add.88), channel_id=1, source_target_pairs={{0,256},{32,288},{64,320},{96,352},{128,384},{160,416},{192,448},{... | collective-permute-start | bytes 4718600 | tf_op jit(solution)/shard_map/ppermute | solution.py:50
  510.5 4.6 copy-start.7
  510.5 26.0 %all-to-all-start.1 = ((f32[8,64,768]{2,1,0:T(8,128)}), f32[8,64,768]{2,1,0:T(8,128)S(1)}, u32[]{:S(2)}, u32[]{:S(2)}) async-start(f32[8,64,768]{2,1,0:T(8,128)} %bitcast.48), calls=%async_computation.1 | async-start | bytes 3145728 | tf_op jit(solution)/shard_map/all_to_all | solution.py:51
  515.3 2.7 copy-start.3
  515.3 2.7 copy-start.6
Sparse Core Ops, SparseCore 0:
  35.8 75.0 all-reduce.3
